TPU v7x, 512 devices: a whole 4x4x16 slice. The times are simulated.
512 devices in a mesh: segment: 16 (over z_lo, x), dp: 8 (over y, core), mp: 4 (over z_hi).
Axes of the slice: x: 4, y: 4, z: 16 (z_hi: 4, z_lo: 4; z = z_hi * 4 + z_lo), core: 2. Of those that a mesh axis runs over, the one named last changes fastest.
Arguments:
- encoder_image_states: bfloat16 [8, 128, 8192], P('dp', 'segment'), may hold values from -6 to 6
- frozen_key_value: bfloat16 [16, 8192, 2, 1024], P('segment', 'dp', None, 'mp'), may hold values from -0.0625 to 0.0625
- adapter_down_weight: bfloat16 [16, 8192, 128], P('segment', 'mp'), may hold values from -0.0625 to 0.0625
- adapter_up_weight: bfloat16 [16, 2, 64, 1024], P('segment', None, None, 'mp'), may hold values from -0.75 to 0.75
- queries: bfloat16 [16, 8, 128, 8192], P('segment', 'dp', None, 'mp'), may hold values from -9 to 9
- cotangent: bfloat16 [16, 8, 128, 8192], P('segment', 'dp', None, 'mp'), may hold values from -1.5 to 1.5
- text_token_length: int32 [8], P('dp'), may hold values from 32 to 128
- image_tile_count: int32 [8], P('dp'), may hold values from 1 to 4
Outputs:
- grad_down: bfloat16 [16, 8192, 128], P('segment', 'mp')
- up_gradient: bfloat16 [16, 2, 64, 1024], P('segment', None, None, 'mp')
- grad_image: float32 [8, 128, 8192], P('dp', 'segment')
All inputs are finite; a program needn't handle non-finite values.
Results may differ from a plain program's by a relative error of at most 0.017.
The roundings to bfloat16 on the way count: a program that leaves them out, or rounds other values in their place, can miss the bound.
Values may be sent and summed in bfloat16 or wider, within the bound.
No kernel may reach another device: no remote copies, remote signals or barrier semaphores. Data moves between devices by JAX's collectives and lax.ppermute only.
A program may use at most 64 MiB of HBM per device.

v0:
```python
import jax
import jax.numpy as jnp
from jax import lax
from jax.sharding import PartitionSpec as P

HD = 128
TILES = 4
adapter_scale = 2.0
contract_rows = (((0,), (0,)), ((), ()))
contracted_columns = (((1,), (1,)), ((), ()))


def body(
    encoder_image_states,
    frozen_key_value,
    adapter_down_weight,
    adapter_up_weight,
    queries,
    cotangent,
    text_token_length,
    image_tile_count,
):
    samples = encoder_image_states.shape[0]
    model_width = encoder_image_states.shape[2]
    whole_img = lax.all_gather(encoder_image_states, "segment", axis=1, tiled=True)
    image_rows = whole_img.shape[1]
    flat_rows = samples * image_rows
    flat_img = whole_img.reshape(flat_rows, model_width)
    fourth_part = adapter_down_weight.shape[1]
    parallel_index = lax.axis_index("mp")
    image_fourth = lax.dynamic_slice_in_dim(flat_img, parallel_index * fourth_part, fourth_part, 1)
    lowrank_state = adapter_up_weight.shape[2]
    key_value_columns = adapter_up_weight.shape[3]
    lowrank_projection = lax.psum(
        jnp.dot(image_fourth, adapter_down_weight[0], preferred_element_type=jnp.float32), "mp"
    ).astype(jnp.bfloat16)
    adapted_weight = jnp.concatenate(
        [
            jnp.dot(
                lowrank_projection[:, :lowrank_state],
                adapter_up_weight[0, 0],
                preferred_element_type=jnp.float32,
            ),
            jnp.dot(
                lowrank_projection[:, lowrank_state:],
                adapter_up_weight[0, 1],
                preferred_element_type=jnp.float32,
            ),
        ],
        axis=1,
    )
    local_weight = frozen_key_value[0]
    full_weight = lax.all_gather(local_weight, "dp", axis=0, tiled=True).reshape(
        model_width, 2 * key_value_columns
    )
    frozen_output = jnp.dot(flat_img, full_weight, preferred_element_type=jnp.float32)
    key_value_pair = (frozen_output + adapter_scale * adapted_weight).astype(jnp.bfloat16)
    local_heads = queries.shape[3] // HD
    local_kv = key_value_columns // HD
    group_size = local_heads // local_kv
    text_rows = queries.shape[2]
    query_rows = queries[0].reshape(samples, text_rows, local_kv, group_size, HD)
    cot_rows = cotangent[0].reshape(samples, text_rows, local_kv, group_size, HD)
    key_rows = key_value_pair[:, :key_value_columns].reshape(samples, image_rows, local_kv, HD)
    value_rows = key_value_pair[:, key_value_columns:].reshape(samples, image_rows, local_kv, HD)
    key_mask = jnp.arange(image_rows, dtype=jnp.int32)[None, :] < image_tile_count[:, None] * (
        image_rows // TILES
    )
    row_mask = (
        jnp.arange(text_rows, dtype=jnp.int32)[None, :] < text_token_length[:, None]
    ).astype(jnp.float32)
    scores = jnp.einsum(
        "btgrd,bjgd->bgrtj", query_rows, key_rows, preferred_element_type=jnp.float32
    ) * HD ** (-0.5)
    masked = jnp.where(key_mask[:, None, None, None, :], scores, -1e30)
    row_top = jnp.max(masked, axis=-1, keepdims=True)
    shifted = jnp.exp(masked - row_top)
    attention = shifted / jnp.sum(shifted, axis=-1, keepdims=True)
    row_gate = row_mask[:, None, None, :, None]
    kept = attention.astype(jnp.bfloat16) * row_gate.astype(jnp.bfloat16)
    dweights = jnp.einsum(
        "btgrd,bjgd->bgrtj", cot_rows, value_rows, preferred_element_type=jnp.float32
    )
    row_delta = jnp.sum(attention * dweights, axis=-1, keepdims=True)
    dscore = (attention * (dweights - row_delta) * row_gate * HD ** (-0.5)).astype(jnp.bfloat16)
    key_grad = jnp.einsum(
        "bgrtj,btgrd->bjgd", dscore, query_rows, preferred_element_type=jnp.float32
    )
    value_grad = jnp.einsum("bgrtj,btgrd->bjgd", kept, cot_rows, preferred_element_type=jnp.float32)
    kv_grad = jnp.concatenate(
        [
            key_grad.reshape(flat_rows, key_value_columns),
            value_grad.reshape(flat_rows, key_value_columns),
        ],
        axis=1,
    ).astype(jnp.bfloat16)
    backward_piece = adapter_scale * jnp.concatenate(
        [
            lax.dot_general(
                kv_grad[:, :key_value_columns],
                adapter_up_weight[0, 0],
                contracted_columns,
                preferred_element_type=jnp.float32,
            ),
            lax.dot_general(
                kv_grad[:, key_value_columns:],
                adapter_up_weight[0, 1],
                contracted_columns,
                preferred_element_type=jnp.float32,
            ),
        ],
        axis=1,
    )
    backward_lowrank = lax.psum(backward_piece, "mp").astype(jnp.bfloat16)
    up_gradient = adapter_scale * jnp.stack(
        [
            lax.dot_general(
                lowrank_projection[:, :lowrank_state],
                kv_grad[:, :key_value_columns],
                contract_rows,
                preferred_element_type=jnp.float32,
            ),
            lax.dot_general(
                lowrank_projection[:, lowrank_state:],
                kv_grad[:, key_value_columns:],
                contract_rows,
                preferred_element_type=jnp.float32,
            ),
        ]
    )
    grad_down = lax.dot_general(
        image_fourth, backward_lowrank, contract_rows, preferred_element_type=jnp.float32
    )
    down_sum, up_sum = lax.psum((grad_down, up_gradient), "dp")
    image_gradient_total = lax.dot_general(
        kv_grad, full_weight, contracted_columns, preferred_element_type=jnp.float32
    )
    adapter_portion = lax.dot_general(
        backward_lowrank,
        adapter_down_weight[0],
        contracted_columns,
        preferred_element_type=jnp.float32,
    )
    current_layer = lax.dynamic_slice_in_dim(
        image_gradient_total, parallel_index * fourth_part, fourth_part, 1
    )
    image_gradient_total = lax.dynamic_update_slice_in_dim(
        image_gradient_total, current_layer + adapter_portion, parallel_index * fourth_part, 1
    )
    image_gradient_total = image_gradient_total.reshape(samples, image_rows, model_width)
    shared_sum = lax.psum_scatter(image_gradient_total, "segment", scatter_dimension=1, tiled=True)
    result = lax.psum(shared_sum, "mp")
    return (down_sum.astype(jnp.bfloat16)[None], up_sum.astype(jnp.bfloat16)[None], result)


def solution(mesh):
    in_specs = (
        P("dp", "segment", None),
        P("segment", "dp", None, "mp"),
        P("segment", "mp", None),
        P("segment", None, None, "mp"),
        P("segment", "dp", None, "mp"),
        P("segment", "dp", None, "mp"),
        P("dp"),
        P("dp"),
    )
    out_specs = (P("segment", "mp", None), P("segment", None, None, "mp"), P("dp", "segment", None))
    return jax.shard_map(body, mesh=mesh, in_specs=in_specs, out_specs=out_specs, check_vma=False)
```

profile of v0, /device:TPU:2, one launch (start us, length us, event | category | flops | bytes accessed | tf_op | source)
XLA Modules:
  0.0 390.2 jit_solution(4577795114373816345)
XLA Ops:
  7.2 0.7 all-gather.4.cloned.1.call-update
  8.0 0.7 all-gather.6.cloned.1.call-update
  10.0 1.3 copy.38
  11.3 2.0 copy.39
  13.4 88.8 %all-gather.4.cloned.1.call-done = bf16[1,128,8192]{2,1,0:T(8,128)(2,1)} async-done(((bf16[1,8,8192]{2,1,0:T(8,128)(2,1)}), bf16[1,128,8192]{2,1,0:T(8,128)(2,1)}) %all-gather.4.cloned.1.call-update) | async-done | bytes 2097168 | tf_op jit(solution)/shard_map/all_gather | solution.py:25
  102.2 1.3 fusion.21
  103.6 25.9 %psum.35 = bf16[128,128]{1,0:T(8,128)(2,1)S(1)} all-reduce(f32[128,128]{1,0:T(8,128)S(1)} %fusion.21), channel_id=1, replica_groups=mesh['segment'=16,'dp'=8,'mp'=4] {'mp'}, use_global_device_ids=true, to_apply=%region_0.0 | all-reduce | flops 16384 | bytes 98304 | tf_op jit(solution)/shard_map/psum | solution.py:34
  129.5 0.2 fusion.42
  129.7 0.1 fusion.46
  129.8 30.6 %all-gather.6.cloned.1.call-done = bf16[1,8192,2,256]{3,2,0,1:T(2,128)(2,1)} async-done(((bf16[1,1024,2,256]{3,2,0,1:T(2,128)(2,1)}), bf16[1,8192,2,256]{3,2,0,1:T(2,128)(2,1)}) %all-gather.6.cloned.1.call-update) | async-done | bytes 8388624 | tf_op jit(solution)/shard_map/all_gather | solution.py:53
  160.5 8.2 %copy.40 = bf16[1024,8,2,256]{3,1,2,0:T(8,128)(2,1)} copy(bf16[1024,8,2,256]{3,2,1,0:T(2,128)(2,1)} %bitcast.113) | data formatting | bytes 16777216
  168.6 4.6 %fusion.10 = bf16[128,512]{1,0:T(8,128)(2,1)S(1)} fusion(bf16[8192,512]{1,0:T(8,128)(2,1)} %bitcast.108, bf16[1,128,8192]{2,1,0:T(8,128)(2,1)S(1)} %copy-done.1, f32[128,256]{1,0:T(8,128)S(1)} %fusion.42, f32[128,256]{1,0:T(8,128)S(1)} %fusion.46), kind=kOutput, calls=%fused_computation.11 | convolution fusion | flops 1074003968 | bytes 10878976 | tf_op jit(solution)/shard_map/dot_general | solution.py:56
  173.3 0.3 fusion.66
  173.6 0.2 fusion.16
  173.8 1.6 fusion.14
  175.4 0.1 fusion.40
  175.6 0.3 multiply_reduce_fusion
  175.9 0.5 fusion.13
  176.4 1.5 slice-done.1
  177.9 4.8 %fusion.34 = f32[128,8192]{1,0:T(8,128)} fusion(bf16[8192,512]{1,0:T(8,128)(2,1)S(1)} %bitcast.111, bf16[128,256]{0,1:T(8,128)(2,1)S(1)} %bitcast.118, bf16[128,256]{0,1:T(8,128)(2,1)S(1)} %bitcast.120), kind=kOutput, calls=%fused_computation.42 | convolution fusion | flops 1074003968 | bytes 12713984 | tf_op jit(solution)/shard_map/dot_general | solution.py:135
  182.7 0.1 fusion.44
  182.8 26.9 %psum.36 = bf16[128,128]{0,1:T(8,128)(2,1)S(1)} all-reduce(f32[128,128]{0,1:T(8,128)S(1)} %maximum_multiply_fusion.2), channel_id=1, replica_groups=mesh['segment'=16,'dp'=8,'mp'=4] {'mp'}, use_global_device_ids=true, to_apply=%region_4.5 | all-reduce | flops 16384 | bytes 98304 | tf_op jit(solution)/shard_map/psum | solution.py:114
  209.8 4.6 %copy.51 = f32[1,128,8192]{2,1,0:T(8,128)} copy(f32[1,128,8192]{2,1,0:T(8,128)} %bitcast.112) | data formatting | bytes 8388608
  214.3 2.5 fusion.1
  216.8 0.0 all-reduce.4.cloned.1.call-start
  216.9 1.3 fusion.23
  218.2 0.2 convolution_bitcast_fusion.3
  218.4 0.2 convolution_bitcast_fusion.4
  218.7 89.1 %reduce-scatter.2.cloned.1.call-done = f32[1,8,8192]{2,1,0:T(8,128)} async-done(((f32[1,128,8192]{2,1,0:T(8,128)}), f32[1,8,8192]{2,1,0:T(8,128)}) %reduce-scatter.2.cloned.1.call-update) | async-done | bytes 262160 | tf_op jit(solution)/shard_map/reduce_scatter | solution.py:151
  307.7 52.3 %all-reduce.5 = (bf16[2048,128]{1,0:T(8,128)(2,1)}, bf16[2,64,256]{2,1,0:T(8,128)(2,1)}) all-reduce(f32[2048,128]{1,0:T(8,128)} %fusion.23, f32[2,64,256]{2,1,0:T(8,128)S(1)} %maximum_multiply_fusion.1), channel_id=1, replica_groups=mesh['segment'=16,'dp'=8,'mp'=4] {'dp'}, use_global_device_ids=true, to_apply=%region_5.6 | all-reduce | flops 294912 | bytes 1769472 | tf_op jit(solution)/shard_map/psum | solution.py:134
  360.0 22.0 %all-reduce.4.cloned.1.call-done = f32[1,8,8192]{2,1,0:T(8,128)} async-done(((f32[1,8,8192]{2,1,0:T(8,128)}), f32[1,8,8192]{2,1,0:T(8,128)}) %all-reduce.4.cloned.1.call-update) | async-done | bytes 262160 | tf_op jit(solution)/shard_map/psum | solution.py:152
  382.0 1.7 copy.57
  (24 shorter events, 0.3 us)
Async XLA Ops:
  7.2 95.1 %copy-start = (bf16[1,2048,128]{2,1,0:T(8,128)(2,1)S(1)}, bf16[1,2048,128]{2,1,0:T(8,128)(2,1)}, u32[]{:S(2)}) copy-start(bf16[1,2048,128]{2,1,0:T(8,128)(2,1)} %param.10) | copy-start | bytes 1572868
  7.2 122.3 %copy-start.3 = (bf16[1,2,64,256]{3,2,1,0:T(8,128)(2,1)S(1)}, bf16[1,2,64,256]{3,2,1,0:T(8,128)(2,1)}, u32[]{:S(2)}) copy-start(bf16[1,2,64,256]{3,2,1,0:T(8,128)(2,1)} %param.11) | copy-start | bytes 196612
  7.2 95.0 %all-gather.4.cloned.1.call-start = ((), (), s32[]{:S(2)}) async-start(), calls=%async_computation.1 | async-start | bytes 2228224 | tf_op jit(solution)/shard_map/all_gather | solution.py:25
  7.9 152.5 %all-gather.6.cloned.1.call-start = ((), (), s32[]{:S(2)}) async-start(), calls=%async_computation.4 | async-start | bytes 9437184 | tf_op jit(solution)/shard_map/all_gather | solution.py:53
  8.7 299.0 %reduce-scatter.2.cloned.1.call-start = ((), (), s32[]{:S(2)}) async-start(), calls=%async_computation.2 | async-start | bytes 4456448 | tf_op jit(solution)/shard_map/reduce_scatter | solution.py:151
  160.5 8.2 %copy-start.1 = (bf16[1,128,8192]{2,1,0:T(8,128)(2,1)S(1)}, bf16[1,128,8192]{2,1,0:T(8,128)(2,1)}, u32[]{:S(2)}) copy-start(bf16[1,128,8192]{2,1,0:T(8,128)(2,1)} %all-gather.4.cloned.1.call-done) | copy-start | bytes 6291460
  173.3 2.2 copy-start.2
  173.8 2.6 slice-start
  175.6 2.4 slice-start.1
  216.8 165.2 %all-reduce.4.cloned.1.call-start = ((), (), s32[]{:S(2)}) async-start(), calls=%async_computation.3 | async-start | bytes 524288 | tf_op jit(solution)/shard_map/psum | solution.py:152
Sparse Core Ops, SparseCore 0:
  10.1 92.1 all-gather.3
  104.4 56.0 all-gather.5
  217.0 90.7 reduce-scatter.1
  310.5 71.4 all-reduce.3
where the time goes:
time: 391 us; the launch traced here: 390 us
  waiting for transfers between devices  232 us (59%)
  blocking collectives  105 us (27%)
  local copies, waits for them, and re-layouts  19.3 us (5%)
  matrix products  18.3 us (5%)
  between operations  15.2 us (4%)
    reduce_scatter x1, waiting for transfers between devices, body(): lax.psum_scatter(image_gradient_total, 'segment', scatter_dimension=1, ti...  89.1 us
    all_gather x1, waiting for transfers between devices, body(): lax.all_gather(encoder_image_states, 'segment', axis=1, tiled=True)  88.8 us
    psum x1, blocking collectives, body(): down_sum, up_sum = lax.psum((grad_down, up_gradient), 'dp')  52.3 us
    all_gather x1, waiting for transfers between devices, body(): lax.all_gather(local_weight, 'dp', axis=0, tiled=True)  30.6 us
    psum x1, blocking collectives, body(): backward_lowrank = lax.psum(backward_piece, 'mp').astype(jnp.bfloat16)  26.9 us
    psum x1, blocking collectives, body(): lax.psum(jnp.dot(image_fourth, adapter_down_weight[0], preferred_element_...  25.9 us
    psum x1, waiting for transfers between devices, body(): result = lax.psum(shared_sum, 'mp')  22 us
    unnamed x15, local copies, waits for them, and re-layouts  15.9 us
  transfers between devices with their start and end apart: 4, of which 4 were waited for; matrix products, arithmetic and copies ran while one was open for 2% of the time, Pallas kernels for 0%

commit v1 on v0

--- a/solution.py
+++ b/solution.py
@@ -149,7 +149,7 @@
     )
     image_gradient_total = image_gradient_total.reshape(samples, image_rows, model_width)
     shared_sum = lax.psum_scatter(image_gradient_total, "segment", scatter_dimension=1, tiled=True)
-    result = lax.psum(shared_sum, "mp")
+    result = jnp.sum(lax.all_gather(shared_sum, "mp"), axis=0)
     return (down_sum.astype(jnp.bfloat16)[None], up_sum.astype(jnp.bfloat16)[None], result)
 
 

time: 391 us -> 381 us (0.974)
  the two profiles are of different devices: /device:TPU:2 before, /device:TPU:1 now
where the time goes in v1:
time: 381 us
  waiting for transfers between devices  218 us (57%)
  blocking collectives  109 us (29%)
  matrix products  18.3 us (5%)
  local copies, waits for them, and re-layouts  17.6 us (5%)
  between operations  15.2 us (4%)
    reduce_scatter x1, waiting for transfers between devices, body(): lax.psum_scatter(image_gradient_total, 'segment', scatter_dimension=1, ti...  87.5 us
    all_gather x1, waiting for transfers between devices, body(): lax.all_gather(encoder_image_states, 'segment', axis=1, tiled=True)  79.7 us
    psum x1, blocking collectives, body(): down_sum, up_sum = lax.psum((grad_down, up_gradient), 'dp')  62.8 us
    all_gather x1, waiting for transfers between devices, body(): lax.all_gather(local_weight, 'dp', axis=0, tiled=True)  44.3 us
    psum x1, blocking collectives, body(): backward_lowrank = lax.psum(backward_piece, 'mp').astype(jnp.bfloat16)  23.9 us
    psum x1, blocking collectives, body(): lax.psum(jnp.dot(image_fourth, adapter_down_weight[0], preferred_element_...  22.6 us
    unnamed x14, local copies, waits for them, and re-layouts  14.2 us
  transfers between devices with their start and end apart: 4, of which 4 were waited for; matrix products, arithmetic and copies ran while one was open for 2% of the time, Pallas kernels for 0%

profile of v1, /device:TPU:1, one launch (start us, length us, event | category | flops | bytes accessed | tf_op | source)
XLA Modules:
  0.0 380.7 jit_solution(15548721168557322286)
XLA Ops:
  7.2 0.7 all-gather.6.cloned.1.call-update
  8.0 0.7 all-gather.8.cloned.1.call-update
  10.0 1.3 copy.38
  11.3 2.0 copy.39
  13.4 79.7 %all-gather.6.cloned.1.call-done = bf16[1,128,8192]{2,1,0:T(8,128)(2,1)} async-done(((bf16[1,8,8192]{2,1,0:T(8,128)(2,1)}), bf16[1,128,8192]{2,1,0:T(8,128)(2,1)}) %all-gather.6.cloned.1.call-update) | async-done | bytes 2097168 | tf_op jit(solution)/shard_map/all_gather | solution.py:25
  93.1 1.3 fusion.21
  94.5 22.6 %psum.28 = bf16[128,128]{1,0:T(8,128)(2,1)S(1)} all-reduce(f32[128,128]{1,0:T(8,128)S(1)} %fusion.21), channel_id=1, replica_groups=mesh['segment'=16,'dp'=8,'mp'=4] {'mp'}, use_global_device_ids=true, to_apply=%region_0.0 | all-reduce | flops 16384 | bytes 98304 | tf_op jit(solution)/shard_map/psum | solution.py:34
  117.1 0.2 fusion.42
  117.3 0.1 fusion.46
  117.4 44.3 %all-gather.8.cloned.1.call-done = bf16[1,8192,2,256]{3,2,0,1:T(2,128)(2,1)} async-done(((bf16[1,1024,2,256]{3,2,0,1:T(2,128)(2,1)}), bf16[1,8192,2,256]{3,2,0,1:T(2,128)(2,1)}) %all-gather.8.cloned.1.call-update) | async-done | bytes 8388624 | tf_op jit(solution)/shard_map/all_gather | solution.py:53
  161.7 8.2 %copy.40 = bf16[1024,8,2,256]{3,1,2,0:T(8,128)(2,1)} copy(bf16[1024,8,2,256]{3,2,1,0:T(2,128)(2,1)} %bitcast.114) | data formatting | bytes 16777216
  169.9 4.6 %fusion.10 = bf16[128,512]{1,0:T(8,128)(2,1)S(1)} fusion(bf16[8192,512]{1,0:T(8,128)(2,1)} %bitcast.109, bf16[1,128,8192]{2,1,0:T(8,128)(2,1)S(1)} %copy-done.1, f32[128,256]{1,0:T(8,128)S(1)} %fusion.42, f32[128,256]{1,0:T(8,128)S(1)} %fusion.46), kind=kOutput, calls=%fused_computation.11 | convolution fusion | flops 1074003968 | bytes 10878976 | tf_op jit(solution)/shard_map/dot_general | solution.py:56
  174.6 0.3 fusion.66
  174.9 0.2 fusion.16
  175.1 1.6 fusion.14
  176.7 0.1 fusion.40
  176.8 0.3 multiply_reduce_fusion
  177.2 0.5 fusion.13
  177.7 1.5 slice-done.1
  179.2 4.8 %fusion.34 = f32[128,8192]{1,0:T(8,128)} fusion(bf16[8192,512]{1,0:T(8,128)(2,1)S(1)} %bitcast.112, bf16[128,256]{0,1:T(8,128)(2,1)S(1)} %bitcast.119, bf16[128,256]{0,1:T(8,128)(2,1)S(1)} %bitcast.121), kind=kOutput, calls=%fused_computation.42 | convolution fusion | flops 1074003968 | bytes 12713984 | tf_op jit(solution)/shard_map/dot_general | solution.py:135
  183.9 0.1 fusion.44
  184.1 23.9 %psum.29 = bf16[128,128]{0,1:T(8,128)(2,1)S(1)} all-reduce(f32[128,128]{0,1:T(8,128)S(1)} %maximum_multiply_fusion.2), channel_id=1, replica_groups=mesh['segment'=16,'dp'=8,'mp'=4] {'mp'}, use_global_device_ids=true, to_apply=%region_4.5 | all-reduce | flops 16384 | bytes 98304 | tf_op jit(solution)/shard_map/psum | solution.py:114
  208.0 4.6 %copy.51 = f32[1,128,8192]{2,1,0:T(8,128)} copy(f32[1,128,8192]{2,1,0:T(8,128)} %bitcast.113) | data formatting | bytes 8388608
  212.6 2.5 fusion.1
  215.1 0.0 all-gather.10.cloned.1.call-start
  215.1 87.5 %reduce-scatter.2.cloned.1.call-done = f32[1,8,8192]{2,1,0:T(8,128)} async-done(((f32[1,128,8192]{2,1,0:T(8,128)}), f32[1,8,8192]{2,1,0:T(8,128)}) %reduce-scatter.2.cloned.1.call-update) | async-done | bytes 262160 | tf_op jit(solution)/shard_map/reduce_scatter | solution.py:151
  302.7 1.4 fusion.23
  304.1 0.2 convolution_bitcast_fusion.3
  304.3 0.2 convolution_bitcast_fusion.4
  304.5 62.8 %all-reduce.2 = (bf16[2048,128]{1,0:T(8,128)(2,1)}, bf16[2,64,256]{2,1,0:T(8,128)(2,1)}) all-reduce(f32[2048,128]{1,0:T(8,128)} %fusion.23, f32[2,64,256]{2,1,0:T(8,128)S(1)} %maximum_multiply_fusion.1), channel_id=1, replica_groups=mesh['segment'=16,'dp'=8,'mp'=4] {'dp'}, use_global_device_ids=true, to_apply=%region_5.6 | all-reduce | flops 294912 | bytes 1769472 | tf_op jit(solution)/shard_map/psum | solution.py:134
  367.3 4.8 %all-gather.10.cloned.1.call-done = f32[4,8,8192]{2,1,0:T(8,128)} async-done(((f32[1,8,8192]{2,1,0:T(8,128)}), f32[4,8,8192]{2,1,0:T(8,128)}) %all-gather.10.cloned.1.call-update) | async-done | bytes 1048592 | tf_op jit(solution)/shard_map/all_gather | solution.py:152
  372.2 2.0 reduce.4
  (24 shorter events, 0.3 us)
Async XLA Ops:
  7.2 86.0 %copy-start = (bf16[1,2048,128]{2,1,0:T(8,128)(2,1)S(1)}, bf16[1,2048,128]{2,1,0:T(8,128)(2,1)}, u32[]{:S(2)}) copy-start(bf16[1,2048,128]{2,1,0:T(8,128)(2,1)} %param.10) | copy-start | bytes 1572868
  7.2 109.9 %copy-start.3 = (bf16[1,2,64,256]{3,2,1,0:T(8,128)(2,1)S(1)}, bf16[1,2,64,256]{3,2,1,0:T(8,128)(2,1)}, u32[]{:S(2)}) copy-start(bf16[1,2,64,256]{3,2,1,0:T(8,128)(2,1)} %param.11) | copy-start | bytes 196612
  7.2 85.9 %all-gather.6.cloned.1.call-start = ((), (), s32[]{:S(2)}) async-start(), calls=%async_computation.1 | async-start | bytes 2228224 | tf_op jit(solution)/shard_map/all_gather | solution.py:25
  7.9 153.8 %all-gather.8.cloned.1.call-start = ((), (), s32[]{:S(2)}) async-start(), calls=%async_computation.3 | async-start | bytes 9437184 | tf_op jit(solution)/shard_map/all_gather | solution.py:53
  8.7 294.0 %reduce-scatter.2.cloned.1.call-start = ((), (), s32[]{:S(2)}) async-start(), calls=%async_computation.2 | async-start | bytes 4456448 | tf_op jit(solution)/shard_map/reduce_scatter | solution.py:151
  161.7 8.2 %copy-start.1 = (bf16[1,128,8192]{2,1,0:T(8,128)(2,1)S(1)}, bf16[1,128,8192]{2,1,0:T(8,128)(2,1)}, u32[]{:S(2)}) copy-start(bf16[1,128,8192]{2,1,0:T(8,128)(2,1)} %all-gather.6.cloned.1.call-done) | copy-start | bytes 6291460
  174.6 2.2 copy-start.2
  175.1 2.6 slice-start
  176.8 2.4 slice-start.1
  215.1 157.1 %all-gather.10.cloned.1.call-start = ((), (), s32[]{:S(2)}) async-start(), calls=%async_computation.4 | async-start | bytes 1310720 | tf_op jit(solution)/shard_map/all_gather | solution.py:152
Sparse Core Ops, SparseCore 0:
  10.1 83.0 all-gather.5
  95.3 66.3 all-gather.7
  215.2 87.4 reduce-scatter.1
  304.6 67.4 all-gather.9
